TPU v7x, 512 devices: a whole 4x4x16 slice. The times are simulated.
512 devices in a mesh: wide: 64 (over z, y_hi, core), narrow: 8 (over x, y_lo).
Axes of the slice: x: 4, y: 4 (y_hi: 2, y_lo: 2; y = y_hi * 2 + y_lo), z: 16, core: 2. Of those that a mesh axis runs over, the one named last changes fastest.
Arguments:
- stiffness: bfloat16 [512, 1024, 1024], P(('wide', 'narrow')), may hold values from -0.125625 to 5, as said below
- load_cases: bfloat16 [512, 1024, 256], P(('wide', 'narrow')), may hold values from -6 to 6
- coarse_inverse: bfloat16 [8192, 8192], P('wide', 'narrow'), may hold values from -0.0011600971 to 0.015625
- face_index: int32 [512, 4, 128], P(('wide', 'narrow')), may hold values from 0 to 1023, as said below
- face_count: int32 [512, 4, 128], P(('wide', 'narrow')), may hold values from 1 to 3, as said below
- aggregate: int32 [512, 1024], P(('wide', 'narrow')), may hold values from 0 to 15
Outputs:
- solution: float32 [512, 1024, 256], P(('wide', 'narrow'))
- coarse: float32 [8192, 256], P(('wide', 'narrow'))
Inputs may be any that keep to these rules, and one draw needn't show every extreme that they name: `face_index`: the 512 entries of one cell are distinct. face_count[c, 1, s] + face_count[c2, 0, s] = 4 where c2 is the cell of the next brick column in the same row, and face_count[c, 3, s] + face_count[c3, 2, s] = 4 where c3 is the cell of the next brick row in the same column. `stiffness`: each cell's matrix is symmetric.
All inputs are finite; a program needn't handle non-finite values.
Results may differ from a plain program's by a relative error of at most 0.018.
Values may be sent and summed in bfloat16 or wider, within the bound.
A program may use at most 64 MiB of HBM per device.

v0:
```python
import jax
import jax.numpy as jnp
from jax import lax
from jax.sharding import PartitionSpec as P

FACE = 128
AGG = 16
CHEB = 4
ITERS = 2


lower_bound = 0.8
upper_bound = 7.5


def extended(block, sides, width):
    for axis, dim in sides:
        count = lax.axis_size(axis)
        forward = [(i, i + 1) for i in range(count - 1)]
        backward = [(target, source) for source, target in forward]
        low = lax.ppermute(
            lax.slice_in_dim(block, block.shape[dim] - width, None, axis=dim), axis, forward
        )
        high = lax.ppermute(lax.slice_in_dim(block, 0, width, axis=dim), axis, backward)
        block = jnp.concatenate([low, block, high], axis=dim)
    return block


def laid_out(parts, dim):
    parts = jnp.moveaxis(parts, 0, dim)
    shape = parts.shape
    return parts.reshape(*shape[:dim], shape[dim] * shape[dim + 1], *shape[dim + 2 :])


def copy_for_each(array, axis):
    copies = jnp.broadcast_to(array, (lax.axis_size(axis), *array.shape))
    return lax.all_to_all(copies, axis, split_axis=0, concat_axis=0, tiled=True)


def collect(array, axis, dim):
    return laid_out(copy_for_each(array, axis), dim)


def split_up(array, dim, peers):
    before, after = (array.shape[:dim], array.shape[dim + 1 :])
    return jnp.moveaxis(array.reshape(*before, peers, -1, *after), dim, 0)


def sent_and_summed(array, axis, dim):
    peers = lax.axis_size(axis)
    parts = lax.all_to_all(split_up(array, dim, peers), axis, 0, 0, tiled=True)
    return jnp.sum(parts.astype(jnp.float32), axis=0)


def chebyshev(matrix, residual):
    center = 0.5 * (upper_bound + lower_bound)
    spread = 0.5 * (upper_bound - lower_bound)
    sigma_ratio = center / spread
    rho_old = 1.0 / sigma_ratio
    direction = residual / center
    result = direction
    remain = residual
    for sweep_index in range(CHEB - 1):
        remain = remain - jnp.dot(
            matrix, direction.astype(jnp.bfloat16), preferred_element_type=jnp.float32
        )
        rho_new = 1.0 / (2.0 * sigma_ratio - rho_old)
        direction = rho_new * rho_old * direction + 2.0 * rho_new / spread * remain
        result = result + direction
        rho_old = rho_new
    return result


def trade_faces(rounded):
    across = extended(rounded[0:2], (("wide", 0),), 1)
    vertical = extended(rounded[2:4], (("narrow", 0),), 1)
    return jnp.stack([across[0], across[3], vertical[0], vertical[3]])


def local(stiffness, load_cases, coarse_inverse, face_index, face_count, aggregate):
    matrix = stiffness[0]
    loads_float = load_cases[0].astype(jnp.float32)
    row_index = face_index[0].reshape(-1)
    column = lax.axis_index("wide")
    brick_row = lax.axis_index("narrow")
    width_count = lax.axis_size("wide")
    height_count = lax.axis_size("narrow")
    present = jnp.stack(
        [column > 0, column < width_count - 1, brick_row > 0, brick_row < height_count - 1]
    )
    present = present.astype(jnp.float32)
    weights = ((4 - face_count[0]).astype(jnp.float32) / 4.0 * present[:, None]).reshape(-1)
    members = jnp.arange(AGG, dtype=jnp.int32)
    onehot = (aggregate[0][None, :] == members[:, None]).astype(jnp.float32)
    solution = jnp.zeros(loads_float.shape, jnp.float32)
    coarse = jnp.zeros((AGG, loads_float.shape[1]), jnp.float32)
    for outer_index in range(ITERS):
        if outer_index == 0:
            residual = loads_float
        else:
            residual = loads_float - jnp.dot(
                matrix, solution.astype(jnp.bfloat16), preferred_element_type=jnp.float32
            )
        coarse_res = jnp.dot(
            onehot, residual, precision=lax.Precision.HIGHEST, preferred_element_type=jnp.float32
        )
        coarse_res = coarse_res.astype(jnp.bfloat16)
        partial_value = jnp.dot(
            coarse_inverse, collect(coarse_res, "wide", 0), preferred_element_type=jnp.float32
        )
        coarse = sent_and_summed(partial_value.astype(jnp.bfloat16), "narrow", 0)
        correction = chebyshev(matrix, residual)
        traces = correction[row_index]
        rounded = traces.astype(jnp.bfloat16).reshape(4, FACE, -1)
        neighbour = trade_faces(rounded).astype(jnp.float32).reshape(4 * FACE, -1)
        blended = traces + weights[:, None] * (neighbour - traces)
        correction = correction.at[row_index].set(blended)
        prolonged = jnp.einsum("ko,kl->ol", onehot, coarse, precision=lax.Precision.HIGHEST)
        solution = solution + correction + prolonged
    return (solution[None], coarse)


def solution(mesh):
    placed = (
        P(("wide", "narrow"), None, None),
        P(("wide", "narrow"), None, None),
        P("wide", "narrow"),
        P(("wide", "narrow"), None, None),
        P(("wide", "narrow"), None, None),
        P(("wide", "narrow"), None),
    )
    return jax.shard_map(
        local,
        mesh=mesh,
        in_specs=placed,
        out_specs=(P(("wide", "narrow"), None, None), P(("wide", "narrow"), None)),
        check_vma=False,
    )
```

profile of v0, /device:TPU:1, one launch (start us, length us, event | category | flops | bytes accessed | tf_op | source)
XLA Modules:
  0.0 126.0 jit_solution(5028861046829925432)
XLA Ops:
  0.7 1.4 %convolution_convert_fusion.3 = bf16[16,256]{1,0:T(8,128)(2,1)S(1)} fusion(bf16[1,1024,256]{2,1,0:T(8,128)(2,1)} %param.7, s32[1024]{0:T(1024)} %bitcast.162), kind=kOutput, calls=%fused_computation.46 | convolution fusion | flops 8409088 | bytes 536576 | tf_op jit(solution)/shard_map/dot_general | solution.py:104
  2.1 0.9 broadcast_in_dim.6
  2.9 20.0 %all-to-all-start = ((bf16[64,16,256]{2,1,0:T(8,128)(2,1)}), bf16[64,16,256]{2,1,0:T(8,128)(2,1)}, u32[]{:S(2)}, u32[]{:S(2)}) async-start(bf16[64,16,256]{2,1,0:T(8,128)(2,1)} %broadcast_in_dim.6), calls=%async_computation | async-start | bytes 1048576 | tf_op jit(solution)/shard_map/all_to_all | solution.py:37
  22.9 0.2 copy.20
  23.1 0.8 convert_subtract_fusion.1
  23.9 0.8 fusion.70
  24.7 2.2 %fusion.67 = f32[1024,256]{0,1:T(8,128)} fusion(f32[1024,256]{0,1:T(8,128)S(1)} %fusion.70, bf16[1,1024,1024]{2,1,0:T(8,128)(2,1)S(1)} %copy-done, f32[1024,256]{0,1:T(8,128)S(1)} %convert_subtract_fusion.1, bf16[1,1024,256]{1,2,0:T(8,128)(2,1)S(1)} %copy.20), kind=kOutput, calls=%fused_computation.41 | convolution fusion | flops 542900224 | bytes 5767168 | tf_op jit(solution)/shard_map/dot_general | solution.py:64
  26.9 1.6 %copy.22 = f32[1024,256]{1,0:T(8,128)S(1)} copy(f32[1024,256]{0,1:T(8,128)} %fusion.67) | data formatting | bytes 2097152 | tf_op jit(solution)/shard_map/add | solution.py:69
  28.6 2.2 %gather_fusion = f32[512,256]{1,0:T(8,128)} fusion(f32[1024,256]{1,0:T(8,128)S(1)} %copy.22, s32[1024]{0:T(1024)S(1)} %pad_clamp_fusion), kind=kCustom, calls=%fused_computation | custom fusion | bytes 1050624 | tf_op jit(solution)/shard_map/gather | solution.py:113
  30.8 1.1 convert_element_type.98
  31.9 0.7 slice_bitcast_fusion.7
  32.6 5.0 %collective-permute-start = (bf16[1,128,256]{2,1,0:T(8,128)(2,1)}, bf16[1,128,256]{2,1,0:T(8,128)(2,1)}, u32[]{:S(2)}, u32[]{:S(2)}) collective-permute-start(bf16[1,128,256]{2,1,0:T(8,128)(2,1)} %get-tuple-element.8), channel_id=1, source_target_pairs={{0,8},{8,16},{16,24},{24,32},{32,40},{40,48},{48,56},{56,64},{64,7... | collective-permute-start | bytes 196616 | tf_op jit(solution)/shard_map/ppermute | solution.py:21
  37.6 1.9 %collective-permute-start.1 = (bf16[1,128,256]{2,1,0:T(8,128)(2,1)}, bf16[1,128,256]{2,1,0:T(8,128)(2,1)}, u32[]{:S(2)}, u32[]{:S(2)}) collective-permute-start(bf16[1,128,256]{2,1,0:T(8,128)(2,1)} %get-tuple-element.11), channel_id=1, source_target_pairs={{8,0},{16,8},{24,16},{32,24},{40,32},{48,40},{56,48},{64,56},{72,6... | collective-permute-start | bytes 196616 | tf_op jit(solution)/shard_map/ppermute | solution.py:24
  39.5 2.9 %collective-permute-start.2 = (bf16[1,128,256]{2,1,0:T(8,128)(2,1)}, bf16[1,128,256]{2,1,0:T(8,128)(2,1)}, u32[]{:S(2)}, u32[]{:S(2)}) collective-permute-start(bf16[1,128,256]{2,1,0:T(8,128)(2,1)} %get-tuple-element.10), channel_id=1, source_target_pairs={{0,1},{1,2},{2,3},{3,4},{4,5},{5,6},{6,7},{8,9},{9,10},{10,11},{11... | collective-permute-start | bytes 196616 | tf_op jit(solution)/shard_map/ppermute | solution.py:21
  42.5 1.3 %collective-permute-start.3 = (bf16[1,128,256]{2,1,0:T(8,128)(2,1)S(1)}, bf16[1,128,256]{2,1,0:T(8,128)(2,1)}, u32[]{:S(2)}, u32[]{:S(2)}) collective-permute-start(bf16[1,128,256]{2,1,0:T(8,128)(2,1)S(1)} %get-tuple-element.9), channel_id=1, source_target_pairs={{1,0},{2,1},{3,2},{4,3},{5,4},{6,5},{7,6},{9,8},{10,9},{11,10},{12... | collective-permute-start | bytes 196616 | tf_op jit(solution)/shard_map/ppermute | solution.py:24
  43.8 0.1 add_select_fusion
  43.9 0.1 bitcast_multiply_fusion
  43.9 12.7 %all-to-all-done = bf16[64,16,256]{2,1,0:T(8,128)(2,1)} async-done(((bf16[64,16,256]{2,1,0:T(8,128)(2,1)}), bf16[64,16,256]{2,1,0:T(8,128)(2,1)}, u32[]{:S(2)}, u32[]{:S(2)}) %all-to-all-start) | async-done | bytes 524320 | tf_op jit(solution)/shard_map/all_to_all | solution.py:37
  56.7 1.9 %convolution_convert_fusion.1 = bf16[256,128]{0,1:T(8,128)(2,1)} fusion(bf16[128,1024]{1,0:T(8,128)(2,1)S(1)} %copy-done.5, bf16[1024,256]{1,0:T(8,128)(2,1)} %bitcast.20), kind=kOutput, calls=%fused_computation.44 | convolution fusion | flops 67141632 | bytes 851968 | tf_op jit(solution)/shard_map/dot_general | solution.py:108
  58.6 4.1 %all-to-all-start.1 = ((bf16[8,16,256]{2,1,0:T(8,128)(2,1)}), bf16[8,16,256]{2,1,0:T(8,128)(2,1)S(1)}, u32[]{:S(2)}, u32[]{:S(2)}) async-start(bf16[8,16,256]{2,1,0:T(8,128)(2,1)} %bitcast.22), calls=%async_computation.1 | async-start | bytes 131072 | tf_op jit(solution)/shard_map/all_to_all | solution.py:51
  62.7 1.7 %pad_maximum_fusion = bf16[4,128,256]{2,1,0:T(8,128)(2,1)} fusion(bf16[1,128,256]{2,1,0:T(8,128)(2,1)} %collective-permute-done.3, bf16[1,128,256]{2,1,0:T(8,128)(2,1)} %collective-permute-done.2, bf16[1,128,256]{2,1,0:T(8,128)(2,1)} %collective-permute-done.1, bf16[1,128,256]{2,1,0:T(8,128)(2,1)} %collective-permute-done), kind=kLoop, calls=%fused_computation.86 | loop fusion | flops 393216 | bytes 524288 | tf_op jit(solution)/shard_map/stack | solution.py:77
  64.4 3.3 %scatter_custom_fusion = f32[1024,256]{1,0:T(8,128)S(1)} fusion(f32[1024,256]{1,0:T(8,128)S(1)} %copy.22, s32[512]{0:T(512)S(1)} %bitcast.167, f32[512,256]{1,0:T(8,128)} %gather_fusion, bf16[512,256]{1,0:T(8,128)(2,1)} %bitcast.161, f32[512]{0:T(512)S(1)} %bitcast_multiply_fusion), kind=kCustom, calls=%fused_computation.68 | custom fusion | flops 524288 | bytes 1837056 | tf_op jit(solution)/shard_map/scatter | solution.py:117
  67.8 0.1 all-to-all-done.1
  67.8 0.6 convolution_add_fusion.1
  68.5 0.4 copy-done.3
  68.9 0.8 convert_subtract_fusion
  69.6 0.2 copy-done.1
  69.8 0.6 convolution_convert_fusion.2
  70.4 0.9 broadcast_in_dim.7
  71.3 7.5 %all-to-all-start.2 = ((bf16[64,16,256]{2,1,0:T(8,128)(2,1)}), bf16[64,16,256]{2,1,0:T(8,128)(2,1)}, u32[]{:S(2)}, u32[]{:S(2)}) async-start(bf16[64,16,256]{2,1,0:T(8,128)(2,1)} %broadcast_in_dim.7), calls=%async_computation.2 | async-start | bytes 1048576 | tf_op jit(solution)/shard_map/all_to_all | solution.py:37
  78.7 0.7 fusion.55
  79.5 0.8 fusion.52
  80.3 2.2 %fusion.49 = f32[1024,256]{0,1:T(8,128)} fusion(f32[1024,256]{0,1:T(8,128)S(1)} %fusion.52, bf16[1,1024,1024]{2,1,0:T(8,128)(2,1)S(1)} %copy-done, f32[1024,256]{0,1:T(8,128)S(1)} %convert_subtract_fusion, f32[1024,256]{0,1:T(8,128)S(1)} %fusion.55), kind=kOutput, calls=%fused_computation.35 | convolution fusion | flops 542375936 | bytes 6291456 | tf_op jit(solution)/shard_map/dot_general | solution.py:64
  82.5 1.6 %copy.24 = f32[1024,256]{1,0:T(8,128)S(1)} copy(f32[1024,256]{0,1:T(8,128)} %fusion.49) | data formatting | bytes 2097152 | tf_op jit(solution)/shard_map/add | solution.py:69
  84.1 2.2 %gather_fusion.1 = f32[512,256]{1,0:T(8,128)} fusion(f32[1024,256]{1,0:T(8,128)S(1)} %copy.24, s32[1024]{0:T(1024)S(1)} %pad_clamp_fusion), kind=kCustom, calls=%fused_computation.1 | custom fusion | bytes 1050624 | tf_op jit(solution)/shard_map/gather | solution.py:113
  86.3 1.1 convert_element_type.109
  87.4 0.7 slice_bitcast_fusion.3
  88.0 5.0 %collective-permute-start.4 = (bf16[1,128,256]{2,1,0:T(8,128)(2,1)}, bf16[1,128,256]{2,1,0:T(8,128)(2,1)}, u32[]{:S(2)}, u32[]{:S(2)}) collective-permute-start(bf16[1,128,256]{2,1,0:T(8,128)(2,1)} %get-tuple-element.4), channel_id=1, source_target_pairs={{0,8},{8,16},{16,24},{24,32},{32,40},{40,48},{48,56},{56,64},{64,7... | collective-permute-start | bytes 196616 | tf_op jit(solution)/shard_map/ppermute | solution.py:21
  93.1 1.9 %collective-permute-start.5 = (bf16[1,128,256]{2,1,0:T(8,128)(2,1)}, bf16[1,128,256]{2,1,0:T(8,128)(2,1)}, u32[]{:S(2)}, u32[]{:S(2)}) collective-permute-start(bf16[1,128,256]{2,1,0:T(8,128)(2,1)} %get-tuple-element.7), channel_id=1, source_target_pairs={{8,0},{16,8},{24,16},{32,24},{40,32},{48,40},{56,48},{64,56},{72,6... | collective-permute-start | bytes 196616 | tf_op jit(solution)/shard_map/ppermute | solution.py:24
  95.0 2.5 %collective-permute-start.6 = (bf16[1,128,256]{2,1,0:T(8,128)(2,1)}, bf16[1,128,256]{2,1,0:T(8,128)(2,1)}, u32[]{:S(2)}, u32[]{:S(2)}) collective-permute-start(bf16[1,128,256]{2,1,0:T(8,128)(2,1)} %get-tuple-element.6), channel_id=1, source_target_pairs={{0,1},{1,2},{2,3},{3,4},{4,5},{5,6},{6,7},{8,9},{9,10},{10,11},{11... | collective-permute-start | bytes 196616 | tf_op jit(solution)/shard_map/ppermute | solution.py:21
  97.5 1.3 %collective-permute-start.7 = (bf16[1,128,256]{2,1,0:T(8,128)(2,1)S(1)}, bf16[1,128,256]{2,1,0:T(8,128)(2,1)}, u32[]{:S(2)}, u32[]{:S(2)}) collective-permute-start(bf16[1,128,256]{2,1,0:T(8,128)(2,1)S(1)} %get-tuple-element.5), channel_id=1, source_target_pairs={{1,0},{2,1},{3,2},{4,3},{5,4},{6,5},{7,6},{9,8},{10,9},{11,10},{12... | collective-permute-start | bytes 196616 | tf_op jit(solution)/shard_map/ppermute | solution.py:24
  98.8 13.7 %all-to-all-done.2 = bf16[64,16,256]{2,1,0:T(8,128)(2,1)} async-done(((bf16[64,16,256]{2,1,0:T(8,128)(2,1)}), bf16[64,16,256]{2,1,0:T(8,128)(2,1)}, u32[]{:S(2)}, u32[]{:S(2)}) %all-to-all-start.2) | async-done | bytes 524320 | tf_op jit(solution)/shard_map/all_to_all | solution.py:37
  112.5 1.9 %convolution_convert_fusion = bf16[256,128]{0,1:T(8,128)(2,1)} fusion(bf16[128,1024]{1,0:T(8,128)(2,1)S(1)} %copy-done.5, bf16[1024,256]{1,0:T(8,128)(2,1)} %bitcast.32), kind=kOutput, calls=%fused_computation.43 | convolution fusion | flops 67141632 | bytes 851968 | tf_op jit(solution)/shard_map/dot_general | solution.py:108
  114.4 3.6 %all-to-all-start.3 = ((bf16[8,16,256]{2,1,0:T(8,128)(2,1)}), bf16[8,16,256]{2,1,0:T(8,128)(2,1)S(1)}, u32[]{:S(2)}, u32[]{:S(2)}) async-start(bf16[8,16,256]{2,1,0:T(8,128)(2,1)} %bitcast.34), calls=%async_computation.3 | async-start | bytes 131072 | tf_op jit(solution)/shard_map/all_to_all | solution.py:51
  118.1 1.0 pad_maximum_fusion.1
  119.0 3.3 %scatter_custom_fusion.1 = f32[1024,256]{1,0:T(8,128)S(1)} fusion(f32[1024,256]{1,0:T(8,128)S(1)} %copy.24, s32[512]{0:T(512)S(1)} %bitcast.168, f32[512,256]{1,0:T(8,128)} %gather_fusion.1, bf16[512,256]{1,0:T(8,128)(2,1)S(1)} %bitcast.160, f32[512]{0:T(512)S(1)} %bitcast_multiply_fusion), kind=kCustom, calls=%fused_computation.64 | custom fusion | flops 524288 | bytes 1837056 | tf_op jit(solution)/shard_map/scatter | solution.py:117
  122.3 0.8 all-to-all-done.3
  123.2 2.8 %fusion.39 = f32[1,1024,256]{2,1,0:T(8,128)} fusion(f32[16,256]{1,0:T(8,128)S(1)} %convert_reduce_fusion, f32[1024,256]{1,0:T(8,128)} %copy-done.1, f32[1024,256]{1,0:T(8,128)S(1)} %scatter_custom_fusion.1, s32[1024]{0:T(1024)S(1)} %bitcast.165), kind=kOutput, calls=%fused_computation.30 | convolution fusion | flops 50872320 | bytes 3166208 | tf_op jit(solution)/shard_map/ko,kl->ol/dot_general | solution.py:118
  (30 shorter events, 0.1 us)
Async XLA Ops:
  0.6 22.5 %copy-start = (bf16[1,1024,1024]{2,1,0:T(8,128)(2,1)S(1)}, bf16[1,1024,1024]{2,1,0:T(8,128)(2,1)}, u32[]{:S(2)}) copy-start(bf16[1,1024,1024]{2,1,0:T(8,128)(2,1)} %param.6) | copy-start | bytes 6291460
  0.6 22.2 %copy-start.4 = (bf16[1,1024,256]{2,1,0:T(8,128)(2,1)S(1)}, bf16[1,1024,256]{2,1,0:T(8,128)(2,1)}, u32[]{:S(2)}) copy-start(bf16[1,1024,256]{2,1,0:T(8,128)(2,1)} %param.7) | copy-start | bytes 1572868
  2.9 53.7 %all-to-all-start = ((bf16[64,16,256]{2,1,0:T(8,128)(2,1)}), bf16[64,16,256]{2,1,0:T(8,128)(2,1)}, u32[]{:S(2)}, u32[]{:S(2)}) async-start(bf16[64,16,256]{2,1,0:T(8,128)(2,1)} %broadcast_in_dim.6), calls=%async_computation | async-start | bytes 1048576 | tf_op jit(solution)/shard_map/all_to_all | solution.py:37
  23.1 1.6 %copy-start.2 = (bf16[1,1024,256]{1,2,0:T(8,128)(2,1)}, bf16[1,1024,256]{1,2,0:T(8,128)(2,1)S(1)}, u32[]{:S(2)}) copy-start(bf16[1,1024,256]{1,2,0:T(8,128)(2,1)S(1)} %copy.20) | copy-start | bytes 1572868
  26.9 1.6 %copy-start.8 = (s32[1,4,128]{2,1,0:T(4,128)S(1)}, s32[1,4,128]{2,1,0:T(4,128)}, u32[]{:S(2)}) copy-start(s32[1,4,128]{2,1,0:T(4,128)} %param.9) | copy-start | bytes 6148
  28.5 15.3 %copy-start.9 = (s32[1,4,128]{2,1,0:T(4,128)S(1)}, s32[1,4,128]{2,1,0:T(4,128)}, u32[]{:S(2)}) copy-start(s32[1,4,128]{2,1,0:T(4,128)} %param.10) | copy-start | bytes 6148
  28.5 28.1 %copy-start.5 = (bf16[128,1024]{1,0:T(8,128)(2,1)S(1)}, bf16[128,1024]{1,0:T(8,128)(2,1)}, u32[]{:S(2)}) copy-start(bf16[128,1024]{1,0:T(8,128)(2,1)} %param.8) | copy-start | bytes 786436
  31.9 36.0 %copy-start.6 = (s32[1,1024]{1,0:T(1,128)S(1)}, s32[1,1024]{1,0:T(1,128)}, u32[]{:S(2)}) copy-start(s32[1,1024]{1,0:T(1,128)} %param.11) | copy-start | bytes 12292
  32.6 30.1 %collective-permute-start = (bf16[1,128,256]{2,1,0:T(8,128)(2,1)}, bf16[1,128,256]{2,1,0:T(8,128)(2,1)}, u32[]{:S(2)}, u32[]{:S(2)}) collective-permute-start(bf16[1,128,256]{2,1,0:T(8,128)(2,1)} %get-tuple-element.8), channel_id=1, source_target_pairs={{0,8},{8,16},{16,24},{24,32},{32,40},{40,48},{48,56},{56,64},{64,7... | collective-permute-start | bytes 196616 | tf_op jit(solution)/shard_map/ppermute | solution.py:21
  37.6 25.1 %collective-permute-start.1 = (bf16[1,128,256]{2,1,0:T(8,128)(2,1)}, bf16[1,128,256]{2,1,0:T(8,128)(2,1)}, u32[]{:S(2)}, u32[]{:S(2)}) collective-permute-start(bf16[1,128,256]{2,1,0:T(8,128)(2,1)} %get-tuple-element.11), channel_id=1, source_target_pairs={{8,0},{16,8},{24,16},{32,24},{40,32},{48,40},{56,48},{64,56},{72,6... | collective-permute-start | bytes 196616 | tf_op jit(solution)/shard_map/ppermute | solution.py:24
  39.5 23.2 %collective-permute-start.2 = (bf16[1,128,256]{2,1,0:T(8,128)(2,1)}, bf16[1,128,256]{2,1,0:T(8,128)(2,1)}, u32[]{:S(2)}, u32[]{:S(2)}) collective-permute-start(bf16[1,128,256]{2,1,0:T(8,128)(2,1)} %get-tuple-element.10), channel_id=1, source_target_pairs={{0,1},{1,2},{2,3},{3,4},{4,5},{5,6},{6,7},{8,9},{9,10},{10,11},{11... | collective-permute-start | bytes 196616 | tf_op jit(solution)/shard_map/ppermute | solution.py:21
  42.5 20.3 %collective-permute-start.3 = (bf16[1,128,256]{2,1,0:T(8,128)(2,1)S(1)}, bf16[1,128,256]{2,1,0:T(8,128)(2,1)}, u32[]{:S(2)}, u32[]{:S(2)}) collective-permute-start(bf16[1,128,256]{2,1,0:T(8,128)(2,1)S(1)} %get-tuple-element.9), channel_id=1, source_target_pairs={{1,0},{2,1},{3,2},{4,3},{5,4},{6,5},{7,6},{9,8},{10,9},{11,10},{12... | collective-permute-start | bytes 196616 | tf_op jit(solution)/shard_map/ppermute | solution.py:24
  58.6 9.2 %all-to-all-start.1 = ((bf16[8,16,256]{2,1,0:T(8,128)(2,1)}), bf16[8,16,256]{2,1,0:T(8,128)(2,1)S(1)}, u32[]{:S(2)}, u32[]{:S(2)}) async-start(bf16[8,16,256]{2,1,0:T(8,128)(2,1)} %bitcast.22), calls=%async_computation.1 | async-start | bytes 131072 | tf_op jit(solution)/shard_map/all_to_all | solution.py:51
  67.8 1.0 copy-start.3
  68.9 1.0 copy-start.1
  71.3 41.2 %all-to-all-start.2 = ((bf16[64,16,256]{2,1,0:T(8,128)(2,1)}), bf16[64,16,256]{2,1,0:T(8,128)(2,1)}, u32[]{:S(2)}, u32[]{:S(2)}) async-start(bf16[64,16,256]{2,1,0:T(8,128)(2,1)} %broadcast_in_dim.7), calls=%async_computation.2 | async-start | bytes 1048576 | tf_op jit(solution)/shard_map/all_to_all | solution.py:37
  88.0 30.0 %collective-permute-start.4 = (bf16[1,128,256]{2,1,0:T(8,128)(2,1)}, bf16[1,128,256]{2,1,0:T(8,128)(2,1)}, u32[]{:S(2)}, u32[]{:S(2)}) collective-permute-start(bf16[1,128,256]{2,1,0:T(8,128)(2,1)} %get-tuple-element.4), channel_id=1, source_target_pairs={{0,8},{8,16},{16,24},{24,32},{32,40},{40,48},{48,56},{56,64},{64,7... | collective-permute-start | bytes 196616 | tf_op jit(solution)/shard_map/ppermute | solution.py:21
  93.1 25.0 %collective-permute-start.5 = (bf16[1,128,256]{2,1,0:T(8,128)(2,1)}, bf16[1,128,256]{2,1,0:T(8,128)(2,1)}, u32[]{:S(2)}, u32[]{:S(2)}) collective-permute-start(bf16[1,128,256]{2,1,0:T(8,128)(2,1)} %get-tuple-element.7), channel_id=1, source_target_pairs={{8,0},{16,8},{24,16},{32,24},{40,32},{48,40},{56,48},{64,56},{72,6... | collective-permute-start | bytes 196616 | tf_op jit(solution)/shard_map/ppermute | solution.py:24
  95.0 23.0 %collective-permute-start.6 = (bf16[1,128,256]{2,1,0:T(8,128)(2,1)}, bf16[1,128,256]{2,1,0:T(8,128)(2,1)}, u32[]{:S(2)}, u32[]{:S(2)}) collective-permute-start(bf16[1,128,256]{2,1,0:T(8,128)(2,1)} %get-tuple-element.6), channel_id=1, source_target_pairs={{0,1},{1,2},{2,3},{3,4},{4,5},{5,6},{6,7},{8,9},{9,10},{10,11},{11... | collective-permute-start | bytes 196616 | tf_op jit(solution)/shard_map/ppermute | solution.py:21
  97.5 20.6 %collective-permute-start.7 = (bf16[1,128,256]{2,1,0:T(8,128)(2,1)S(1)}, bf16[1,128,256]{2,1,0:T(8,128)(2,1)}, u32[]{:S(2)}, u32[]{:S(2)}) collective-permute-start(bf16[1,128,256]{2,1,0:T(8,128)(2,1)S(1)} %get-tuple-element.5), channel_id=1, source_target_pairs={{1,0},{2,1},{3,2},{4,3},{5,4},{6,5},{7,6},{9,8},{10,9},{11,10},{12... | collective-permute-start | bytes 196616 | tf_op jit(solution)/shard_map/ppermute | solution.py:24
  114.4 8.7 %all-to-all-start.3 = ((bf16[8,16,256]{2,1,0:T(8,128)(2,1)}), bf16[8,16,256]{2,1,0:T(8,128)(2,1)S(1)}, u32[]{:S(2)}, u32[]{:S(2)}) async-start(bf16[8,16,256]{2,1,0:T(8,128)(2,1)} %bitcast.34), calls=%async_computation.3 | async-start | bytes 131072 | tf_op jit(solution)/shard_map/all_to_all | solution.py:51
  123.1 2.8 %copy-start.7 = (f32[16,256]{1,0:T(8,128)}, f32[16,256]{1,0:T(8,128)S(1)}, u32[]{:S(2)}) copy-start(f32[16,256]{1,0:T(8,128)S(1)} %convert_reduce_fusion) | copy-start | bytes 49156
where the time goes:
time: 128 us; the launch traced here: 126 us
  starting transfers between devices  57 us (45%)
  waiting for transfers between devices  27.4 us (21%)
  matrix products  17.5 us (14%)
  other arithmetic  11.6 us (9%)
  local copies, waits for them, and re-layouts  11.5 us (9%)
    all_to_all x2, starting transfers between devices, copy_for_each(): return lax.all_to_all(copies, axis, split_axis=0, concat_axis=0, tiled=True)  27.4 us
    all_to_all x2, waiting for transfers between devices, copy_for_each(): return lax.all_to_all(copies, axis, split_axis=0, concat_axis=0, tiled=True)  26.5 us
    ppermute x4, starting transfers between devices, extended(): lax.ppermute(lax.slice_in_dim(block, block.shape[dim] - width, None, axis...  15.5 us
    all_to_all x2, starting transfers between devices, sent_and_summed(): parts = lax.all_to_all(split_up(array, dim, peers), axis, 0, 0, tiled=True)  7.74 us
    dot_general x6, matrix products, chebyshev(): jnp.dot(matrix, direction.astype(jnp.bfloat16), preferred_element_type=jn...  7.5 us
    scatter x2, other arithmetic, local(): correction = correction.at[row_index].set(blended)  6.6 us
    ppermute x4, starting transfers between devices, extended(): lax.ppermute(lax.slice_in_dim(block, 0, width, axis=dim), axis, backward)  6.4 us
    gather x2, local copies, waits for them, and re-layouts, local(): traces = correction[row_index]  4.46 us
  transfers between devices with their start and end apart: 12, of which 4 were waited for; matrix products, arithmetic and copies ran while one was open for 25% of the time, Pallas kernels for 0%

commit v1 on v0

v1 whole, which is shorter than its diff:
```python
import jax
import jax.numpy as jnp
from jax import lax
from jax.experimental import pallas as pl
from jax.experimental.pallas import tpu as pltpu
from jax.sharding import PartitionSpec as P

ORDER = 1024
FACE = 128
AGG = 16
LOADS = 256
CHEB = 4
DEPTH = 16
CLASSES = 4
ROWS = 8
GROUP = CLASSES * ROWS
CHUNK = 256

lower_bound = 0.8
upper_bound = 7.5
center = 0.5 * (upper_bound + lower_bound)
spread = 0.5 * (upper_bound - lower_bound)

f32 = jnp.float32
bf16 = jnp.bfloat16


def steps():
    sigma_ratio = center / spread
    rho_old = 1.0 / sigma_ratio
    factors = []
    for _ in range(CHEB - 1):
        rho_new = 1.0 / (2.0 * sigma_ratio - rho_old)
        factors.append((rho_new * rho_old, 2.0 * rho_new / spread))
        rho_old = rho_new
    return factors


FACTORS = steps()


def offsets():
    every = [(a, b, c) for a in range(4) for b in range(4) for c in range(2)]
    every = [o for o in every if o != (0, 0, 0)]
    return sorted(every, key=lambda o: -(min(o[0], 4 - o[0]) + min(o[1], 4 - o[1])))


OFFSETS = offsets()


def dot(a, b):
    return jnp.dot(a, b, preferred_element_type=f32)


def over_rows(body, size=CHUNK, total=ORDER):
    @pl.loop(0, total // size)
    def _(i):
        body(pl.ds(pl.multiple_of(i * size, size), size))


def split(value):
    high = value.astype(bf16)
    return high, (value - high.astype(f32)).astype(bf16)


def transposed_row(row):
    return jnp.transpose(jnp.broadcast_to(row.astype(f32), (128, 128)))


def fill_prolongation(agg_ref, into):
    lane = lax.broadcasted_iota(jnp.int32, (128, 128), 1)
    member = jnp.where(lane < 2 * AGG, lane % AGG, -1).astype(f32)
    for i in range(ORDER // 128):
        column = transposed_row(agg_ref[:, i * 128 : (i + 1) * 128])
        into[i * 128 : (i + 1) * 128, :] = jnp.where(column == member, 1.0, 0.0).astype(bf16)


def kernel(
    stiffness, loads, inverse, face_index, face_count, aggregate,
    y_ref, coarse_ref,
    K, B, A, q, d, zs, x1, da, db, G, Gw, D, Pm, Pt, PK, S,
    aperm, A2, v1, v2, ys1, ys2, r1, r2, t1, t2, n1, n2, C, pb,
    lsem, asem, arecv, vsend, vrecv, ysend, yrecv, tsend, trecv, osem,
):
    w = lax.axis_index("wide")
    n = lax.axis_index("narrow")
    z = w // 4
    cls = w % 4
    y = ((w // 2) % 2) * 2 + n % 2
    x = n // 2
    core = w % 2

    def along(k):
        return (((z + DEPTH + k) % DEPTH) * 4 + cls, n)

    def depth_rows(k):
        return pl.ds(pl.multiple_of(((z + DEPTH + k) % DEPTH) * AGG, AGG), AGG)

    def member(o):
        yy = (y + o[1]) % 4
        other = (yy // 2) * 2 + (core + o[2]) % 2
        nn = ((x + o[0]) % 4) * 2 + yy % 2
        return (z * 4 + other, nn), other * ROWS + nn

    def group_rows(index):
        return pl.ds(pl.multiple_of(index * AGG, AGG), AGG)

    own = cls * ROWS + n
    sides = [((w + 63) % 64, n), ((w + 1) % 64, n), (w, (n + 7) % 8), (w, (n + 1) % 8)]

    barrier = pltpu.get_barrier_semaphore()
    near = [along(s * k) for k in (4, 3, 2, 1) for s in (1, -1)]
    greeted = near + [member(o)[0] for o in OFFSETS] + sides[:2]
    for peer in greeted:
        pl.semaphore_signal(barrier, inc=1, device_id=peer, device_id_type=pl.DeviceIdType.MESH)

    load_b = pltpu.make_async_copy(loads, B, lsem.at[0])
    load_a = pltpu.make_async_copy(inverse, A, lsem.at[1])
    load_k = pltpu.make_async_copy(stiffness, K, lsem.at[2])
    load_b.start()
    load_a.start()
    load_k.start()

    def send(src, dst, ssem, rsem, peer):
        pltpu.make_async_remote_copy(
            src_ref=src, dst_ref=dst, send_sem=ssem, recv_sem=rsem,
            device_id=peer, device_id_type=pl.DeviceIdType.MESH,
        ).start()

    def wait(ref, sem):
        pltpu.make_async_copy(ref, ref, sem).wait()

    sub16 = lax.broadcasted_iota(jnp.int32, (AGG, ORDER), 0)
    Pm[...] = jnp.where(sub16 == aggregate[...], 1.0, 0.0).astype(bf16)
    load_b.wait()
    first = dot(Pm[...], B[...])
    pb[...] = first
    v1[depth_rows(0), :] = first.astype(bf16)

    load_a.wait()
    for j in range(CLASSES):
        place = lax.broadcasted_iota(jnp.int32, (CHUNK, CHUNK), 1)
        place = (place // AGG) * (CLASSES * AGG) + j * AGG + place % AGG
        row = lax.broadcasted_iota(jnp.int32, (CHUNK, CHUNK), 0)
        total = jnp.zeros((128, CHUNK), f32)
        for t in range(4):
            pick = jnp.where(row + t * CHUNK == place, 1.0, 0.0).astype(bf16)
            total = total + dot(A[:, t * CHUNK : (t + 1) * CHUNK], pick)
        aperm[j] = total.astype(bf16)
    A2[cls] = aperm[cls]

    pl.semaphore_wait(barrier, len(greeted))

    for i, k in enumerate((4, -4, 3, -3, 2, -2, 1, -1)):
        sem = vrecv.at[0] if k == 4 else vrecv.at[1] if k == -4 else vrecv.at[2]
        send(v1.at[depth_rows(0)], v1.at[depth_rows(0)], vsend.at[0], sem, along(k))
    for k in (1, 2, 3):
        other = (cls + k) % 4
        send(aperm.at[other], A2.at[cls], asem, arecv, (z * 4 + other, n))

    lane = lax.broadcasted_iota(jnp.int32, (128, 128), 1).astype(f32)
    sub = lax.broadcasted_iota(jnp.int32, (128, 128), 0).astype(f32)
    there = [w > 0, w < 63, n > 0, n < 7]
    for f in range(4):
        row = face_index[f : f + 1, :].astype(f32)
        column = transposed_row(row)
        weight = (4 - face_count[f : f + 1, :]).astype(f32) * 0.25
        weight = weight * jnp.where(there[f], 1.0, 0.0)
        for i in range(8):
            hit = jnp.where(column == lane + 128.0 * i, 1.0, 0.0)
            G[f * 128 : (f + 1) * 128, i * 128 : (i + 1) * 128] = hit.astype(bf16)
            hit = jnp.where(row == sub + 128.0 * i, weight, 0.0)
            Gw[i * 128 : (i + 1) * 128, f * 128 : (f + 1) * 128] = hit.astype(bf16)

    def chebyshev(after_second):
        def start(rows):
            da[rows, :] = (q[rows, :] * (1.0 / center)).astype(bf16)

        over_rows(start)
        for s, (keep, gain) in enumerate(FACTORS):
            src, dst = (da, db) if s % 2 == 0 else (db, da)

            def step(rows, s=s, keep=keep, gain=gain, src=src, dst=dst):
                before = q[rows, :]
                left = before - dot(K[rows, :], src[...])
                old = before * (1.0 / center) if s == 0 else d[rows, :]
                result = old if s == 0 else zs[rows, :]
                new = keep * old + gain * left
                if s < CHEB - 2:
                    q[rows, :] = left
                    d[rows, :] = new
                zs[rows, :] = result + new
                dst[rows, :] = (new if s < CHEB - 2 else result + new).astype(bf16)

            over_rows(step)
            if s == 1:
                after_second()
        return db

    def trade(corr, t, nb, tsem, rsem):
        t[...] = dot(G[...], corr[...]).astype(bf16)
        for f, target in ((0, 1), (1, 0), (2, 3), (3, 2)):
            send(
                t.at[pl.ds(f * FACE, FACE)], nb.at[pl.ds(target * FACE, FACE)], tsem, rsem,
                sides[f],
            )

    def relay():
        wait(v1.at[depth_rows(-4)], vrecv.at[0])
        for k in (4, 3, 2, 1):
            send(v1.at[depth_rows(-4)], v1.at[depth_rows(-4)], vsend.at[0], vrecv.at[2], along(k))
        wait(v1.at[depth_rows(4)], vrecv.at[1])
        for k in (-3, -2, -1):
            send(v1.at[depth_rows(4)], v1.at[depth_rows(4)], vsend.at[0], vrecv.at[2], along(k))

    def scatter_partials(v, ys, r, ssem, rsem):
        for half in range(2):
            rows = pl.ds(half * CHUNK, CHUNK)
            value = dot(A2[2 * half : 2 * half + 2].reshape(CHUNK, CHUNK), v[...])
            ys[rows, :] = value.astype(bf16)
        for o in OFFSETS:
            peer, index = member(o)
            send(ys.at[group_rows(index)], r.at[group_rows(own)], ssem, rsem, peer)
        r[group_rows(own), :] = ys[group_rows(own), :]

    def gathered_sum(r):
        total = r[0:AGG, :].astype(f32)
        for i in range(1, GROUP):
            total = total + r[i * AGG : (i + 1) * AGG, :].astype(f32)
        return total

    def to_f32(rows):
        q[rows, :] = B[rows, :].astype(f32)

    over_rows(to_f32)
    load_k.wait()
    corr = chebyshev(relay)
    trade(corr, t1, n1, tsend.at[0], trecv.at[0])

    fill_prolongation(aggregate, Pt)
    high, low = split(dot(Pm[...], K[...]))
    PK[0:AGG, :] = high
    PK[AGG : 2 * AGG, :] = low
    both = dot(PK[...], Pt[...])
    high, low = split(both[0:AGG] + both[AGG : 2 * AGG])
    S[0:AGG, :] = high
    S[AGG : 2 * AGG, :] = low
    C[2 * AGG :, :] = jnp.zeros((128 - 2 * AGG, LOADS), bf16)

    wait(v1.at[pl.ds(0, 13 * AGG)], vrecv.at[2])
    wait(A2.at[pl.ds(0, 3)], arecv)
    scatter_partials(v1, ys1, r1, ysend.at[0], yrecv.at[0])

    def keep_share(rows):
        D[rows, :] = 1.0 - dot(Gw[rows, :], jnp.ones((4 * FACE, LOADS), bf16))

    over_rows(keep_share)
    wait(n1, trecv.at[0])

    def average(rows):
        value = D[rows, :] * zs[rows, :] + dot(Gw[rows, :], n1[...])
        x1[rows, :] = value
        da[rows, :] = value.astype(bf16)

    over_rows(average)
    both = dot(PK[...], da[...])
    pb[...] = pb[...] - both[0:AGG] - both[AGG : 2 * AGG]

    wait(r1.at[pl.ds(0, (GROUP - 1) * AGG)], yrecv.at[0])
    high, low = split(gathered_sum(r1))
    C[0:AGG, :] = high
    C[AGG : 2 * AGG, :] = low
    both = dot(S[...], C[...])
    v2[depth_rows(0), :] = (pb[...] - both[0:AGG] - both[AGG : 2 * AGG]).astype(bf16)
    for k in (8, 7, -7, 6, -6, 5, -5, 4, -4, 3, -3, 2, -2, 1, -1):
        send(v2.at[depth_rows(0)], v2.at[depth_rows(0)], vsend.at[1], vrecv.at[3], along(k))

    def prolong(rows):
        value = x1[rows, :] + dot(Pt[rows, :], C[...])
        x1[rows, :] = value
        db[rows, :] = value.astype(bf16)

    over_rows(prolong)

    def residual(rows):
        q[rows, :] = B[rows, :].astype(f32) - dot(K[rows, :], db[...])

    over_rows(residual)
    corr = chebyshev(lambda: None)
    trade(corr, t2, n2, tsend.at[1], trecv.at[1])
    wait(v2.at[pl.ds(0, 15 * AGG)], vrecv.at[3])
    scatter_partials(v2, ys2, r2, ysend.at[1], yrecv.at[1])
    wait(n2, trecv.at[1])

    def finish(rows):
        value = D[rows, :] * zs[rows, :] + dot(Gw[rows, :], n2[...])
        x1[rows, :] = x1[rows, :] + value

    over_rows(finish)
    out = pltpu.make_async_copy(x1, y_ref, osem)
    out.start()
    wait(r2.at[pl.ds(0, (GROUP - 1) * AGG)], yrecv.at[1])
    coarse_ref[...] = gathered_sum(r2)
    out.wait()

    wait(v1.at[pl.ds(0, 15 * AGG)], vsend.at[0])
    wait(aperm.at[pl.ds(0, 3)], asem)
    wait(t1, tsend.at[0])
    wait(ys1.at[pl.ds(0, (GROUP - 1) * AGG)], ysend.at[0])
    wait(v2.at[pl.ds(0, 15 * AGG)], vsend.at[1])
    wait(t2, tsend.at[1])
    wait(ys2.at[pl.ds(0, (GROUP - 1) * AGG)], ysend.at[1])


def closing(y_ref, coarse_ref, aggregate, out_ref, out_coarse, Pt, C):
    i = pl.program_id(0)

    @pl.when(i == 0)
    def _():
        fill_prolongation(aggregate, Pt)
        high, low = split(coarse_ref[...])
        C[0:AGG, :] = high
        C[AGG : 2 * AGG, :] = low
        C[2 * AGG :, :] = jnp.zeros((128 - 2 * AGG, LOADS), bf16)
        out_coarse[...] = coarse_ref[...]

    rows = pl.ds(pl.multiple_of(i * CHUNK, CHUNK), CHUNK)
    out_ref[...] = y_ref[...] + dot(Pt[rows, :], C[...])


def local(stiffness, load_cases, coarse_inverse, face_index, face_count, aggregate):
    vmem = pl.BlockSpec(memory_space=pltpu.VMEM)
    anywhere = pl.BlockSpec(memory_space=pl.ANY)
    wide_f32 = pltpu.VMEM((ORDER, LOADS), f32)
    wide_bf16 = pltpu.VMEM((ORDER, LOADS), bf16)
    square = pltpu.VMEM((CHUNK, LOADS), bf16)
    half = pltpu.VMEM((GROUP * AGG, LOADS), bf16)
    dma = pltpu.SemaphoreType.DMA
    y, coarse = pl.pallas_call(
        kernel,
        out_shape=(
            jax.ShapeDtypeStruct((ORDER, LOADS), f32),
            jax.ShapeDtypeStruct((AGG, LOADS), f32),
        ),
        in_specs=[anywhere, anywhere, anywhere, vmem, vmem, vmem],
        out_specs=(anywhere, vmem),
        scratch_shapes=[
            pltpu.VMEM((ORDER, ORDER), bf16),
            wide_bf16,
            pltpu.VMEM((128, ORDER), bf16),
            wide_f32, wide_f32, wide_f32, wide_f32,
            wide_bf16, wide_bf16,
            pltpu.VMEM((4 * FACE, ORDER), bf16),
            pltpu.VMEM((ORDER, 4 * FACE), bf16),
            wide_f32,
            pltpu.VMEM((AGG, ORDER), bf16),
            pltpu.VMEM((ORDER, 128), bf16),
            pltpu.VMEM((2 * AGG, ORDER), bf16),
            pltpu.VMEM((2 * AGG, 128), bf16),
            pltpu.VMEM((CLASSES, 128, CHUNK), bf16),
            pltpu.VMEM((CLASSES, 128, CHUNK), bf16),
            square, square,
            half, half, half, half, half, half, half, half,
            pltpu.VMEM((128, LOADS), bf16),
            pltpu.VMEM((AGG, LOADS), f32),
            dma((3,)), dma, dma, dma((2,)), dma((4,)),
            dma((2,)), dma((2,)), dma((2,)), dma((2,)), dma,
        ],
        compiler_params=pltpu.CompilerParams(
            collective_id=0, has_side_effects=True, vmem_limit_bytes=60 * 2**20
        ),
        name="schwarz",
    )(stiffness[0], load_cases[0], coarse_inverse, face_index[0], face_count[0], aggregate)

    whole = pl.BlockSpec((AGG, LOADS), lambda i: (0, 0))
    block = pl.BlockSpec((CHUNK, LOADS), lambda i: (i, 0))
    result, coarse = pl.pallas_call(
        closing,
        grid=(ORDER // CHUNK,),
        out_shape=(
            jax.ShapeDtypeStruct((ORDER, LOADS), f32),
            jax.ShapeDtypeStruct((AGG, LOADS), f32),
        ),
        in_specs=[block, whole, pl.BlockSpec((1, ORDER), lambda i: (0, 0))],
        out_specs=(block, whole),
        scratch_shapes=[pltpu.VMEM((ORDER, 128), bf16), pltpu.VMEM((128, LOADS), bf16)],
        name="closing",
    )(y, coarse, aggregate)
    return (result[None], coarse)


def solution(mesh):
    both = ("wide", "narrow")
    placed = (
        P(both, None, None),
        P(both, None, None),
        P("wide", "narrow"),
        P(both, None, None),
        P(both, None, None),
        P(both, None),
    )
    return jax.shard_map(
        local,
        mesh=mesh,
        in_specs=placed,
        out_specs=(P(both, None, None), P(both, None)),
        check_vma=False,
    )
```

time: 128 us -> 53.5 us (0.42); the launches traced: 126 us -> 53.3 us
  starting transfers between devices: 57 us -> 0 us
  Pallas kernels: 0 us -> 52.6 us
  waiting for transfers between devices: 27.4 us -> 0 us
  matrix products: 17.5 us -> 0 us
  other arithmetic: 11.6 us -> 0 us
  local copies, waits for them, and re-layouts: 11.5 us -> 0 us
    pallas_call x0 -> x2, Pallas kernels: none -> 52.6 us  [the longest x1 48.7 us: local(): pl.pallas_call(kernel, out_shape=(jax.ShapeDtypeStruct((ORDER, LOADS), f3...]
    all_to_all x4 -> x0, starting transfers between devices: 35.1 us -> none  [the longest x2 27.4 us: copy_for_each(): return lax.all_to_all(copies, axis, split_axis=0, concat_axis=0, tiled=True)]
    all_to_all x4 -> x0, waiting for transfers between devices: 27.4 us -> none  [the longest x2 26.5 us: copy_for_each(): return lax.all_to_all(copies, axis, split_axis=0, concat_axis=0, tiled=True)]
    ppermute x8 -> x0, starting transfers between devices: 21.9 us -> none  [the longest x4 15.5 us: extended(): lax.ppermute(lax.slice_in_dim(block, block.shape[dim] - width, None, axis...]
    dot_general x13 -> x0, matrix products: 17.5 us -> none  [the longest x6 7.5 us: chebyshev(): jnp.dot(matrix, direction.astype(jnp.bfloat16), preferred_element_type=jn...]
    scatter x2 -> x0, other arithmetic: 6.6 us -> none  [local(): correction = correction.at[row_index].set(blended)]
    gather x2 -> x0, local copies, waits for them, and re-layouts: 4.46 us -> none  [local(): traces = correction[row_index]]
    add x2 -> x0, local copies, waits for them, and re-layouts: 3.12 us -> none  [chebyshev(): result = result + direction]
  transfers between devices with their start and end apart: 12 -> 0, of which waited for: 4 -> 0; matrix products, arithmetic and copies ran while one was open for 25% -> 0% of each run, Pallas kernels for 0% -> 0%
where the time goes in v1:
time: 53.5 us; the launch traced here: 53.3 us
  Pallas kernels  52.6 us (98%)
  between operations  0.64 us (1%)
    pallas_call x1, Pallas kernels, local(): pl.pallas_call(kernel, out_shape=(jax.ShapeDtypeStruct((ORDER, LOADS), f3...  48.7 us
    pallas_call x1, Pallas kernels, local(): pl.pallas_call(closing, grid=(ORDER // CHUNK,), out_shape=(jax.ShapeDtype...  3.9 us

profile of v1, /device:TPU:1, one launch (start us, length us, event | category | flops | bytes accessed | tf_op | source)
XLA Modules:
  0.0 53.3 jit_solution(6839578959407018718)
XLA Ops:
  0.6 48.7 %schwarz.1 = (f32[1024,256]{1,0:T(8,128)}, f32[16,256]{1,0:T(8,128)}) custom-call(bf16[1024,1024]{1,0:T(8,128)(2,1)} %bitcast.5, bf16[1024,256]{1,0:T(8,128)(2,1)} %bitcast.6, bf16[128,1024]{1,0:T(8,128)(2,1)} %inverse.1, s32[4,128]{1,0:T(4,128)} %bitcast.7, s32[4,128]{1,0:T(4,128)} %bitcast.8, s32[1,1024]{1,0:T(1,128)} %aggregate.3), custom_call_target="tpu_custom_call" | custom-call | tf_op jit(solution)/shard_map/schwarz/pallas_call | solution.py:339
  49.4 3.9 %closing.1 = (f32[1024,256]{1,0:T(8,128)}, f32[16,256]{1,0:T(8,128)}) custom-call(f32[1024,256]{1,0:T(8,128)} %get-tuple-element.6.y_ref, f32[16,256]{1,0:T(8,128)} %get-tuple-element.7.coarse_ref, s32[1,1024]{1,0:T(1,128)} %aggregate.3), custom_call_target="tpu_custom_call" | custom-call | tf_op jit(solution)/shard_map/closing/pallas_call | solution.py:377

commit v2 on v1

v2 whole, which is shorter than its diff:
```python
import jax
import jax.numpy as jnp
from jax import lax
from jax.experimental import pallas as pl
from jax.experimental.pallas import tpu as pltpu
from jax.sharding import PartitionSpec as P

ORDER = 1024
FACE = 128
AGG = 16
LOADS = 256
CHEB = 4
DEPTH = 16
CLASSES = 4
ROWS = 8
GROUP = 2 * ROWS
CHUNK = 256

lower_bound = 0.8
upper_bound = 7.5
center = 0.5 * (upper_bound + lower_bound)
spread = 0.5 * (upper_bound - lower_bound)

f32 = jnp.float32
bf16 = jnp.bfloat16


def steps():
    sigma_ratio = center / spread
    rho_old = 1.0 / sigma_ratio
    factors = []
    for _ in range(CHEB - 1):
        rho_new = 1.0 / (2.0 * sigma_ratio - rho_old)
        factors.append((rho_new * rho_old, 2.0 * rho_new / spread))
        rho_old = rho_new
    return factors


FACTORS = steps()


def offsets():
    every = [(a, b) for a in range(4) for b in range(4) if (a, b) != (0, 0)]
    return sorted(every, key=lambda o: -(min(o[0], 4 - o[0]) + min(o[1], 4 - o[1])))


OFFSETS = offsets()


def dot(a, b):
    return jnp.dot(a, b, preferred_element_type=f32)


def over_rows(body, size=CHUNK, total=ORDER):
    for i in range(total // size):
        body(slice(i * size, (i + 1) * size))


def split(value):
    high = value.astype(bf16)
    return high, (value - high.astype(f32)).astype(bf16)


def transposed_row(row):
    return jnp.transpose(jnp.broadcast_to(row.astype(f32), (128, 128)))


def fill_prolongation(agg_ref, into):
    lane = lax.broadcasted_iota(jnp.int32, (128, 128), 1)
    member = jnp.where(lane < 2 * AGG, lane % AGG, -1).astype(f32)
    for i in range(ORDER // 128):
        column = transposed_row(agg_ref[:, i * 128 : (i + 1) * 128])
        into[i * 128 : (i + 1) * 128, :] = jnp.where(column == member, 1.0, 0.0).astype(bf16)


def kernel(
    stiffness, loads, inverse, indices, counts, groups,
    y_ref, pt_ref, c_ref, coarse_ref,
    K, B, A, q, d, zs, x1, da, db, G, Gw, D, Pm, Pt, PK, S,
    aggregate, face_index, face_count, aperm, A2, v1, v2, ys1, ys2, r1, r2, t1, t2, n1, n2, C, pb,
    lsem, asem, arecv, vsend, vrecv, csend, crecv, ysend, yrecv, tsend, trecv,
):
    load_b = pltpu.make_async_copy(loads, B, lsem.at[0])
    load_k = pltpu.make_async_copy(stiffness, K, lsem.at[2])
    load_a = pltpu.make_async_copy(inverse, A, lsem.at[1])
    load_g = pltpu.make_async_copy(groups, aggregate, lsem.at[3])
    load_i = pltpu.make_async_copy(indices, face_index, lsem.at[4])
    load_c = pltpu.make_async_copy(counts, face_count, lsem.at[5])
    load_g.start()
    load_b.start()

    w = lax.axis_index("wide")
    n = lax.axis_index("narrow")
    z = w // 4
    y = ((w // 2) % 2) * 2 + n % 2
    x = n // 2
    high = (w // 2) % 2
    core = w % 2

    def along(k):
        return (((z + DEPTH + k) % DEPTH) * 4 + high * 2 + core, n)

    def slot(k):
        return pl.ds((k % DEPTH) * AGG, AGG)

    def member(o):
        yy = (y + o[1]) % 4
        nn = ((x + o[0]) % 4) * 2 + yy % 2
        return (z * 4 + (yy // 2) * 2 + core, nn), (yy // 2) * ROWS + nn

    def group_rows(index):
        return pl.ds(pl.multiple_of(index * AGG, AGG), AGG)

    own = high * ROWS + n
    other_core = (z * 4 + high * 2 + 1 - core, n)
    across = (z * 4 + (1 - high) * 2 + core, n)
    sides = [((w + 63) % 64, n), ((w + 1) % 64, n), (w, (n + 7) % 8), (w, (n + 1) % 8)]

    barrier = pltpu.get_barrier_semaphore()
    greeted = [along(s * k) for k in (4, 3, 2, 1) for s in (1, -1)]
    greeted = greeted + [member(o)[0] for o in OFFSETS] + sides[:2] + [other_core]
    for peer in greeted:
        pl.semaphore_signal(barrier, inc=1, device_id=peer, device_id_type=pl.DeviceIdType.MESH)
    load_k.start()
    load_a.start()
    load_i.start()
    load_c.start()

    def send(src, dst, ssem, rsem, peer):
        pltpu.make_async_remote_copy(
            src_ref=src, dst_ref=dst, send_sem=ssem, recv_sem=rsem,
            device_id=peer, device_id_type=pl.DeviceIdType.MESH,
        ).start()

    def wait(ref, sem):
        pltpu.make_async_copy(ref, ref, sem).wait()

    load_g.wait()
    sub16 = lax.broadcasted_iota(jnp.int32, (AGG, ORDER), 0)
    Pm[...] = jnp.where(sub16 == aggregate[...], 1.0, 0.0).astype(bf16)
    load_b.wait()
    first = dot(Pm[...], B[...])
    v1[core, slot(0), :] = first.astype(bf16)
    pb[...] = first

    pl.semaphore_wait(barrier, len(greeted))

    for k in (4, -4, 3, -3, 2, -2, 1, -1):
        sem = vrecv.at[0] if k == 4 else vrecv.at[1] if k == -4 else vrecv.at[2]
        send(v1.at[core, slot(0)], v1.at[core, slot(-k)], vsend.at[0], sem, along(k))

    load_a.wait()
    for j in range(CLASSES):
        place = lax.broadcasted_iota(jnp.int32, (CHUNK, CHUNK), 1)
        place = ((place // AGG + z) % DEPTH) * (CLASSES * AGG) + j * AGG + place % AGG
        row = lax.broadcasted_iota(jnp.int32, (CHUNK, CHUNK), 0)
        total = jnp.zeros((128, CHUNK), f32)
        for t in range(4):
            pick = jnp.where(row + t * CHUNK == place, 1.0, 0.0).astype(bf16)
            total = total + dot(A[:, t * CHUNK : (t + 1) * CHUNK], pick)
        aperm[j // 2, j % 2] = total.astype(bf16)
    send(aperm.at[1 - high], A2.at[high], asem, arecv, across)
    A2[high] = aperm[high]

    def chebyshev(after_second):
        def begin(rows):
            da[rows, :] = (q[rows, :] * (1.0 / center)).astype(bf16)

        over_rows(begin)
        for s, (keep, gain) in enumerate(FACTORS):
            src, dst = (da, db) if s % 2 == 0 else (db, da)

            def step(rows, s=s, keep=keep, gain=gain, src=src, dst=dst):
                before = q[rows, :]
                left = before - dot(K[rows, :], src[...])
                old = before * (1.0 / center) if s == 0 else d[rows, :]
                result = old if s == 0 else zs[rows, :]
                new = keep * old + gain * left
                if s < CHEB - 2:
                    q[rows, :] = left
                    d[rows, :] = new
                zs[rows, :] = result + new
                dst[rows, :] = (new if s < CHEB - 2 else result + new).astype(bf16)

            over_rows(step)
            if s == 1:
                after_second()
        return db

    def trade(corr, t, nb, tsem, rsem):
        t[...] = dot(G[...], corr[...]).astype(bf16)
        for f, target in ((0, 1), (1, 0), (2, 3), (3, 2)):
            send(
                t.at[pl.ds(f * FACE, FACE)], nb.at[pl.ds(target * FACE, FACE)], tsem, rsem,
                sides[f],
            )

    def relay():
        wait(v1.at[core, slot(-4)], vrecv.at[0])
        for k in (4, 3, 2, 1):
            send(v1.at[core, slot(-4)], v1.at[core, slot(-4 - k)], vsend.at[0], vrecv.at[3], along(k))
        wait(v1.at[core, slot(4)], vrecv.at[1])
        for k in (3, 2, 1):
            send(v1.at[core, slot(4)], v1.at[core, slot(4 + k)], vsend.at[0], vrecv.at[3], along(-k))

    def share(v, first_slot, count, ssem, rsem):
        rows = pl.ds(first_slot * AGG, count * AGG)
        send(v.at[core, rows], v.at[core, rows], ssem, rsem, other_core)

    def coarse_product(v, ys, r, near, nears, far, ssem, rsem, i):
        wait(v.at[core, pl.ds(0, nears * AGG)], vrecv.at[near])
        share(v, 0, 5, csend.at[i], crecv.at[i])
        share(v, 12, 4, csend.at[i], crecv.at[i])
        wait(v.at[core, pl.ds(0, 7 * AGG)], vrecv.at[far])
        share(v, 5, 7, csend.at[i], crecv.at[i])
        if i == 0:
            wait(A2.at[0], arecv)
        mine = dot(A2[:, core].reshape(CHUNK, CHUNK), v[core])
        wait(v.at[core], crecv.at[i])
        value = mine + dot(A2[:, 1 - core].reshape(CHUNK, CHUNK), v[1 - core])
        ys[...] = value.astype(bf16)
        for o in OFFSETS:
            peer, index = member(o)
            send(ys.at[group_rows(index)], r.at[group_rows(own)], ssem, rsem, peer)
        r[group_rows(own), :] = ys[group_rows(own), :]

    def gathered_sum(r):
        total = r[0:AGG, :].astype(f32)
        for i in range(1, GROUP):
            total = total + r[i * AGG : (i + 1) * AGG, :].astype(f32)
        return total

    def to_f32(rows):
        q[rows, :] = B[rows, :].astype(f32)

    over_rows(to_f32)
    load_k.wait()
    corr = chebyshev(relay)

    load_i.wait()
    load_c.wait()
    lane = lax.broadcasted_iota(jnp.int32, (128, 128), 1).astype(f32)
    sub = lax.broadcasted_iota(jnp.int32, (128, 128), 0).astype(f32)
    there = [w > 0, w < 63, n > 0, n < 7]
    for f in range(4):
        row = face_index[f : f + 1, :].astype(f32)
        column = transposed_row(row)
        weight = (4 - face_count[f : f + 1, :]).astype(f32) * 0.25
        weight = weight * jnp.where(there[f], 1.0, 0.0)
        for i in range(8):
            hit = jnp.where(column == lane + 128.0 * i, 1.0, 0.0)
            G[f * 128 : (f + 1) * 128, i * 128 : (i + 1) * 128] = hit.astype(bf16)
            hit = jnp.where(row == sub + 128.0 * i, weight, 0.0)
            Gw[i * 128 : (i + 1) * 128, f * 128 : (f + 1) * 128] = hit.astype(bf16)
    trade(corr, t1, n1, tsend.at[0], trecv.at[0])

    fill_prolongation(aggregate, Pt)
    top, low = split(dot(Pm[...], K[...]))
    PK[0:AGG, :] = top
    PK[AGG : 2 * AGG, :] = low
    both = dot(PK[...], Pt[...])
    top, low = split(both[0:AGG] + both[AGG : 2 * AGG])
    S[0:AGG, :] = top
    S[AGG : 2 * AGG, :] = low
    C[2 * AGG :, :] = jnp.zeros((128 - 2 * AGG, LOADS), bf16)
    pt_ref[...] = Pt[...]

    coarse_product(v1, ys1, r1, 2, 6, 3, ysend.at[0], yrecv.at[0], 0)

    def keep_share(rows):
        D[rows, :] = 1.0 - dot(Gw[rows, :], jnp.ones((4 * FACE, LOADS), bf16))

    over_rows(keep_share)
    wait(n1, trecv.at[0])

    def average(rows):
        value = D[rows, :] * zs[rows, :] + dot(Gw[rows, :], n1[...])
        x1[rows, :] = value
        da[rows, :] = value.astype(bf16)

    over_rows(average)
    both = dot(PK[...], da[...])
    pb[...] = pb[...] - both[0:AGG] - both[AGG : 2 * AGG]

    wait(r1.at[pl.ds(0, (GROUP - 1) * AGG)], yrecv.at[0])
    top, low = split(gathered_sum(r1))
    C[0:AGG, :] = top
    C[AGG : 2 * AGG, :] = low
    both = dot(S[...], C[...])
    v2[core, slot(0), :] = (pb[...] - both[0:AGG] - both[AGG : 2 * AGG]).astype(bf16)
    for k in (8, 7, -7, 6, -6, 5, -5, 4, -4, 3, -3, 2, -2, 1, -1):
        sem = vrecv.at[4] if abs(k) <= 4 else vrecv.at[5]
        send(v2.at[core, slot(0)], v2.at[core, slot(-k)], vsend.at[1], sem, along(k))

    def prolong(rows):
        value = x1[rows, :] + dot(Pt[rows, :], C[...])
        x1[rows, :] = value
        db[rows, :] = value.astype(bf16)

    over_rows(prolong)

    def residual(rows):
        q[rows, :] = B[rows, :].astype(f32) - dot(K[rows, :], db[...])

    over_rows(residual)
    corr = chebyshev(lambda: None)
    trade(corr, t2, n2, tsend.at[1], trecv.at[1])
    coarse_product(v2, ys2, r2, 4, 8, 5, ysend.at[1], yrecv.at[1], 1)
    wait(n2, trecv.at[1])

    def finish(rows):
        value = D[rows, :] * zs[rows, :] + dot(Gw[rows, :], n2[...])
        y_ref[rows, :] = x1[rows, :] + value

    over_rows(finish)
    wait(r2.at[pl.ds(0, (GROUP - 1) * AGG)], yrecv.at[1])
    total = gathered_sum(r2)
    top, low = split(total)
    c_ref[0:AGG, :] = top
    c_ref[AGG : 2 * AGG, :] = low
    c_ref[2 * AGG :, :] = jnp.zeros((128 - 2 * AGG, LOADS), bf16)
    coarse_ref[...] = total

    wait(v1.at[core, pl.ds(0, 15 * AGG)], vsend.at[0])
    wait(aperm.at[0], asem)
    wait(t1, tsend.at[0])
    wait(v1.at[core], csend.at[0])
    wait(ys1.at[pl.ds(0, (GROUP - 1) * AGG)], ysend.at[0])
    wait(v2.at[core, pl.ds(0, 15 * AGG)], vsend.at[1])
    wait(v2.at[core], csend.at[1])
    wait(t2, tsend.at[1])
    wait(ys2.at[pl.ds(0, (GROUP - 1) * AGG)], ysend.at[1])


def closing(y_ref, pt_ref, c_ref, coarse_ref, out_ref, out_coarse, ys, osem):
    out_coarse[...] = coarse_ref[...]
    gives = []
    for i in range(ORDER // CHUNK):
        rows = pl.ds(i * CHUNK, CHUNK)
        ys[rows, :] = y_ref[rows, :] + dot(pt_ref[rows, :], c_ref[...])
        copy = pltpu.make_async_copy(ys.at[rows], out_ref.at[rows], osem.at[i])
        copy.start()
        gives.append(copy)
    for copy in gives:
        copy.wait()


def local(stiffness, load_cases, coarse_inverse, face_index, face_count, aggregate):
    vmem = pl.BlockSpec(memory_space=pltpu.VMEM)
    anywhere = pl.BlockSpec(memory_space=pl.ANY)
    wide_f32 = pltpu.VMEM((ORDER, LOADS), f32)
    wide_bf16 = pltpu.VMEM((ORDER, LOADS), bf16)
    square = pltpu.VMEM((CHUNK, LOADS), bf16)
    pair = pltpu.VMEM((2, CHUNK, LOADS), bf16)
    faces = pltpu.VMEM((4 * FACE, LOADS), bf16)
    hbm = pl.BlockSpec(memory_space=pltpu.HBM)
    dma = pltpu.SemaphoreType.DMA
    y, pt, c, coarse = pl.pallas_call(
        kernel,
        out_shape=(
            jax.ShapeDtypeStruct((ORDER, LOADS), f32),
            jax.ShapeDtypeStruct((ORDER, 128), bf16),
            jax.ShapeDtypeStruct((128, LOADS), bf16),
            jax.ShapeDtypeStruct((AGG, LOADS), f32),
        ),
        in_specs=[hbm, hbm, hbm, hbm, hbm, hbm],
        out_specs=(vmem, vmem, vmem, vmem),
        scratch_shapes=[
            pltpu.VMEM((ORDER, ORDER), bf16),
            wide_bf16,
            pltpu.VMEM((128, ORDER), bf16),
            wide_f32, wide_f32, wide_f32, wide_f32,
            wide_bf16, wide_bf16,
            pltpu.VMEM((4 * FACE, ORDER), bf16),
            pltpu.VMEM((ORDER, 4 * FACE), bf16),
            wide_f32,
            pltpu.VMEM((AGG, ORDER), bf16),
            pltpu.VMEM((ORDER, 128), bf16),
            pltpu.VMEM((2 * AGG, ORDER), bf16),
            pltpu.VMEM((2 * AGG, 128), bf16),
            pltpu.VMEM((1, ORDER), jnp.int32),
            pltpu.VMEM((4, FACE), jnp.int32),
            pltpu.VMEM((4, FACE), jnp.int32),
            pltpu.VMEM((2, 2, 128, CHUNK), bf16),
            pltpu.VMEM((2, 2, 128, CHUNK), bf16),
            pair, pair,
            square, square, square, square, faces, faces, faces, faces,
            pltpu.VMEM((128, LOADS), bf16),
            pltpu.VMEM((AGG, LOADS), f32),
            dma((6,)), dma, dma, dma((2,)), dma((6,)), dma((2,)), dma((2,)),
            dma((2,)), dma((2,)), dma((2,)), dma((2,)),
        ],
        compiler_params=pltpu.CompilerParams(
            collective_id=0, has_side_effects=True, vmem_limit_bytes=24 * 2**20
        ),
        name="schwarz",
    )(*[pltpu.with_memory_space_constraint(v, pltpu.HBM) for v in (stiffness[0], load_cases[0], coarse_inverse, face_index[0], face_count[0], aggregate)])
    result, coarse = pl.pallas_call(
        closing,
        out_shape=(
            jax.ShapeDtypeStruct((ORDER, LOADS), f32),
            jax.ShapeDtypeStruct((AGG, LOADS), f32),
        ),
        in_specs=[vmem, vmem, vmem, vmem],
        out_specs=(anywhere, vmem),
        scratch_shapes=[wide_f32, dma((4,))],
        compiler_params=pltpu.CompilerParams(vmem_limit_bytes=8 * 2**20),
        name="closing",
    )(y, pt, c, coarse)
    return (result[None], coarse)


def solution(mesh):
    both = ("wide", "narrow")
    placed = (
        P(both, None, None),
        P(both, None, None),
        P("wide", "narrow"),
        P(both, None, None),
        P(both, None, None),
        P(both, None),
    )
    return jax.shard_map(
        local,
        mesh=mesh,
        in_specs=placed,
        out_specs=(P(both, None, None), P(both, None)),
        check_vma=False,
    )
```

time: 53.5 us -> 48.7 us (0.910)
  Pallas kernels: 52.6 us -> 47.9 us
    pallas_call x1, Pallas kernels: 48.7 us -> 46.1 us  [local(): pl.pallas_call(kernel, out_shape=(jax.ShapeDtypeStruct((ORDER, LOADS), f3...]
    pallas_call x1, Pallas kernels: 3.9 us -> 1.83 us  [local(): pl.pallas_call(closing, out_shape=(jax.ShapeDtypeStruct((ORDER, LOADS), f...]
where the time goes in v2:
time: 48.7 us; the launch traced here: 48.6 us
  Pallas kernels  47.9 us (98%)
  between operations  0.64 us (1%)
    pallas_call x1, Pallas kernels, local(): pl.pallas_call(kernel, out_shape=(jax.ShapeDtypeStruct((ORDER, LOADS), f3...  46.1 us
    pallas_call x1, Pallas kernels, local(): pl.pallas_call(closing, out_shape=(jax.ShapeDtypeStruct((ORDER, LOADS), f...  1.83 us

profile of v2, /device:TPU:1, one launch (start us, length us, event | category | flops | bytes accessed | tf_op | source)
XLA Modules:
  0.0 48.6 jit_solution(15377561846861884881)
XLA Ops:
  0.6 46.1 %schwarz.1 = (f32[1024,256]{1,0:T(8,128)S(1)}, bf16[1024,128]{1,0:T(8,128)(2,1)S(1)}, bf16[128,256]{1,0:T(8,128)(2,1)S(1)}, f32[16,256]{1,0:T(8,128)S(1)}) custom-call(bf16[1024,1024]{1,0:T(8,128)(2,1)} %bitcast.5, bf16[1024,256]{1,0:T(8,128)(2,1)} %bitcast.6, bf16[128,1024]{1,0:T(8,128)(2,1)} %inverse.1, s32[4,128]{1,0:T(4,128)} %bitcast.7, ...), custom_call_target="tpu_custom_call" | custom-call | tf_op jit(solution)/shard_map/schwarz/pallas_call | solution.py:358
  46.7 1.8 %closing.1 = (f32[1024,256]{1,0:T(8,128)}, f32[16,256]{1,0:T(8,128)}) custom-call(f32[1024,256]{1,0:T(8,128)S(1)} %get-tuple-element.8.y_ref, bf16[1024,128]{1,0:T(8,128)(2,1)S(1)} %get-tuple-element.9.pt_ref, bf16[128,256]{1,0:T(8,128)(2,1)S(1)} %get-tuple-element.10.c_ref, f32[16,256]{1,0:T(8,128)S(1)} %get-tuple-element.11.coarse_ref), custom_call_target="tpu_custom_call" | custom-call | tf_op jit(solution)/shard_map/closing/pallas_call | solution.py:398

commit v3 on v2

--- a/solution.py
+++ b/solution.py
@@ -14,6 +14,8 @@
 CLASSES = 4
 ROWS = 8
 GROUP = 2 * ROWS
+HALF = LOADS // 2
+BLOCK = 2 * AGG
 CHUNK = 256
 
 lower_bound = 0.8
@@ -40,7 +42,8 @@
 
 
 def offsets():
-    every = [(a, b) for a in range(4) for b in range(4) if (a, b) != (0, 0)]
+    every = [(a, b, c) for a in range(4) for b in range(4) for c in range(2)]
+    every = [o for o in every if o != (0, 0, 0)]
     return sorted(every, key=lambda o: -(min(o[0], 4 - o[0]) + min(o[1], 4 - o[1])))
 
 
@@ -77,8 +80,8 @@
     stiffness, loads, inverse, indices, counts, groups,
     y_ref, pt_ref, c_ref, coarse_ref,
     K, B, A, q, d, zs, x1, da, db, G, Gw, D, Pm, Pt, PK, S,
-    aggregate, face_index, face_count, aperm, A2, v1, v2, ys1, ys2, r1, r2, t1, t2, n1, n2, C, pb,
-    lsem, asem, arecv, vsend, vrecv, csend, crecv, ysend, yrecv, tsend, trecv,
+    aggregate, face_index, face_count, aperm, A2, u1, u2, v1, v2, ys1, ys2, r1, r2, t1, t2, n1, n2, C, pb,
+    lsem, asem, arecv, vsend, vrecv, ysend, yrecv, tsend, trecv,
 ):
     load_b = pltpu.make_async_copy(loads, B, lsem.at[0])
     load_k = pltpu.make_async_copy(stiffness, K, lsem.at[2])
@@ -97,28 +100,33 @@
     high = (w // 2) % 2
     core = w % 2
 
-    def along(k):
-        return (((z + DEPTH + k) % DEPTH) * 4 + high * 2 + core, n)
+    def along(k, c=None):
+        c = core if c is None else c
+        return (((z + DEPTH + k) % DEPTH) * 4 + high * 2 + c, n)
 
     def slot(k):
-        return pl.ds((k % DEPTH) * AGG, AGG)
+        return pl.ds((k % DEPTH) * BLOCK, BLOCK)
+
+    def part(k, c):
+        return pl.ds(pl.multiple_of((k % DEPTH) * BLOCK + c * AGG, AGG), AGG)
 
     def member(o):
         yy = (y + o[1]) % 4
+        cc = (core + o[2]) % 2
         nn = ((x + o[0]) % 4) * 2 + yy % 2
-        return (z * 4 + (yy // 2) * 2 + core, nn), (yy // 2) * ROWS + nn
+        up = yy // 2
+        return (z * 4 + up * 2 + cc, nn), (up * 2 + cc) * ROWS + nn
 
     def group_rows(index):
         return pl.ds(pl.multiple_of(index * AGG, AGG), AGG)
 
-    own = high * ROWS + n
-    other_core = (z * 4 + high * 2 + 1 - core, n)
-    across = (z * 4 + (1 - high) * 2 + core, n)
+    cls = high * 2 + core
+    own = core * GROUP + high * ROWS + n
     sides = [((w + 63) % 64, n), ((w + 1) % 64, n), (w, (n + 7) % 8), (w, (n + 1) % 8)]
 
     barrier = pltpu.get_barrier_semaphore()
-    greeted = [along(s * k) for k in (4, 3, 2, 1) for s in (1, -1)]
-    greeted = greeted + [member(o)[0] for o in OFFSETS] + sides[:2] + [other_core]
+    greeted = [along(s * k, c) for k in (4, 3, 2, 1) for s in (1, -1) for c in (0, 1)]
+    greeted = greeted + [member(o)[0] for o in OFFSETS] + sides[:2]
     for peer in greeted:
         pl.semaphore_signal(barrier, inc=1, device_id=peer, device_id_type=pl.DeviceIdType.MESH)
     load_k.start()
@@ -140,27 +148,43 @@
     Pm[...] = jnp.where(sub16 == aggregate[...], 1.0, 0.0).astype(bf16)
     load_b.wait()
     first = dot(Pm[...], B[...])
-    v1[core, slot(0), :] = first.astype(bf16)
     pb[...] = first
 
+    def offer(u, v, value, i):
+        for c in range(2):
+            u[c] = value[:, c * HALF : (c + 1) * HALF].astype(bf16)
+        v[part(0, core), :] = u[core]
+
+    def spread(u, v, distances, sem_of, i):
+        for k in distances:
+            for c in range(2):
+                send(u.at[c], v.at[part(-k, core)], vsend.at[i], sem_of(k), along(k, c))
+        send(u.at[1 - core], v.at[part(0, core)], vsend.at[i], sem_of(0), along(0, 1 - core))
+
+    offer(u1, v1, first, 0)
     pl.semaphore_wait(barrier, len(greeted))
 
-    for k in (4, -4, 3, -3, 2, -2, 1, -1):
-        sem = vrecv.at[0] if k == 4 else vrecv.at[1] if k == -4 else vrecv.at[2]
-        send(v1.at[core, slot(0)], v1.at[core, slot(-k)], vsend.at[0], sem, along(k))
+    def first_sem(k):
+        return vrecv.at[0] if k == 4 else vrecv.at[1] if k == -4 else vrecv.at[2]
+
+    spread(u1, v1, (4, -4, 3, -3, 2, -2, 1, -1), first_sem, 0)
 
     load_a.wait()
-    for j in range(CLASSES):
-        place = lax.broadcasted_iota(jnp.int32, (CHUNK, CHUNK), 1)
-        place = ((place // AGG + z) % DEPTH) * (CLASSES * AGG) + j * AGG + place % AGG
-        row = lax.broadcasted_iota(jnp.int32, (CHUNK, CHUNK), 0)
-        total = jnp.zeros((128, CHUNK), f32)
-        for t in range(4):
-            pick = jnp.where(row + t * CHUNK == place, 1.0, 0.0).astype(bf16)
-            total = total + dot(A[:, t * CHUNK : (t + 1) * CHUNK], pick)
-        aperm[j // 2, j % 2] = total.astype(bf16)
-    send(aperm.at[1 - high], A2.at[high], asem, arecv, across)
-    A2[high] = aperm[high]
+    for j in range(2):
+        for part_of in range(2):
+            place = lax.broadcasted_iota(jnp.int32, (CHUNK, CHUNK), 1) + part_of * CHUNK
+            place = ((place // BLOCK + z) % DEPTH) * (2 * BLOCK) + j * BLOCK + place % BLOCK
+            row = lax.broadcasted_iota(jnp.int32, (CHUNK, CHUNK), 0)
+            total = jnp.zeros((128, CHUNK), f32)
+            for t in range(4):
+                pick = jnp.where(row + t * CHUNK == place, 1.0, 0.0).astype(bf16)
+                total = total + dot(A[:, t * CHUNK : (t + 1) * CHUNK], pick)
+            aperm[j, :, part_of * CHUNK : (part_of + 1) * CHUNK] = total.astype(bf16)
+    for up, c in ((1, 1), (1, 0), (0, 1)):
+        hh = (high + up) % 2
+        target = (z * 4 + hh * 2 + (core + c) % 2, n)
+        send(aperm.at[hh], A2.at[cls], asem, arecv, target)
+    A2[cls] = aperm[high]
 
     def chebyshev(after_second):
         def begin(rows):
@@ -196,39 +220,33 @@
             )
 
     def relay():
-        wait(v1.at[core, slot(-4)], vrecv.at[0])
+        wait(v1.at[slot(-4)], vrecv.at[0])
         for k in (4, 3, 2, 1):
-            send(v1.at[core, slot(-4)], v1.at[core, slot(-4 - k)], vsend.at[0], vrecv.at[3], along(k))
-        wait(v1.at[core, slot(4)], vrecv.at[1])
+            send(v1.at[slot(-4)], v1.at[slot(-4 - k)], vsend.at[0], vrecv.at[2], along(k))
+        wait(v1.at[slot(4)], vrecv.at[1])
         for k in (3, 2, 1):
-            send(v1.at[core, slot(4)], v1.at[core, slot(4 + k)], vsend.at[0], vrecv.at[3], along(-k))
-
-    def share(v, first_slot, count, ssem, rsem):
-        rows = pl.ds(first_slot * AGG, count * AGG)
-        send(v.at[core, rows], v.at[core, rows], ssem, rsem, other_core)
-
-    def coarse_product(v, ys, r, near, nears, far, ssem, rsem, i):
-        wait(v.at[core, pl.ds(0, nears * AGG)], vrecv.at[near])
-        share(v, 0, 5, csend.at[i], crecv.at[i])
-        share(v, 12, 4, csend.at[i], crecv.at[i])
-        wait(v.at[core, pl.ds(0, 7 * AGG)], vrecv.at[far])
-        share(v, 5, 7, csend.at[i], crecv.at[i])
+            send(v1.at[slot(4)], v1.at[slot(4 + k)], vsend.at[0], vrecv.at[2], along(-k))
+
+    def coarse_product(v, ys, r, blocks, vsem, ssem, rsem, i):
+        wait(v.at[pl.ds(0, blocks * AGG)], vsem)
         if i == 0:
-            wait(A2.at[0], arecv)
-        mine = dot(A2[:, core].reshape(CHUNK, CHUNK), v[core])
-        wait(v.at[core], crecv.at[i])
-        value = mine + dot(A2[:, 1 - core].reshape(CHUNK, CHUNK), v[1 - core])
-        ys[...] = value.astype(bf16)
+            wait(A2.at[pl.ds(0, 3)], arecv)
+        for j in range(2):
+            value = dot(A2[2 * j : 2 * j + 2].reshape(CHUNK, 2 * CHUNK), v[...])
+            ys[j * CHUNK : (j + 1) * CHUNK, :] = value.astype(bf16)
         for o in OFFSETS:
             peer, index = member(o)
             send(ys.at[group_rows(index)], r.at[group_rows(own)], ssem, rsem, peer)
-        r[group_rows(own), :] = ys[group_rows(own), :]
+        r[group_rows(own), :] = ys[group_rows(cls * ROWS + n), :]
 
     def gathered_sum(r):
-        total = r[0:AGG, :].astype(f32)
-        for i in range(1, GROUP):
-            total = total + r[i * AGG : (i + 1) * AGG, :].astype(f32)
-        return total
+        halves = []
+        for c in range(2):
+            total = r[c * CHUNK : c * CHUNK + AGG, :].astype(f32)
+            for i in range(1, GROUP):
+                total = total + r[c * CHUNK + i * AGG : c * CHUNK + (i + 1) * AGG, :].astype(f32)
+            halves.append(total)
+        return jnp.concatenate(halves, axis=1)
 
     def to_f32(rows):
         q[rows, :] = B[rows, :].astype(f32)
@@ -265,7 +283,7 @@
     C[2 * AGG :, :] = jnp.zeros((128 - 2 * AGG, LOADS), bf16)
     pt_ref[...] = Pt[...]
 
-    coarse_product(v1, ys1, r1, 2, 6, 3, ysend.at[0], yrecv.at[0], 0)
+    coarse_product(v1, ys1, r1, 27, vrecv.at[2], ysend.at[0], yrecv.at[0], 0)
 
     def keep_share(rows):
         D[rows, :] = 1.0 - dot(Gw[rows, :], jnp.ones((4 * FACE, LOADS), bf16))
@@ -282,15 +300,21 @@
     both = dot(PK[...], da[...])
     pb[...] = pb[...] - both[0:AGG] - both[AGG : 2 * AGG]
 
-    wait(r1.at[pl.ds(0, (GROUP - 1) * AGG)], yrecv.at[0])
+    wait(r1.at[pl.ds(0, (2 * GROUP - 1) * AGG)], yrecv.at[0])
     top, low = split(gathered_sum(r1))
     C[0:AGG, :] = top
     C[AGG : 2 * AGG, :] = low
     both = dot(S[...], C[...])
-    v2[core, slot(0), :] = (pb[...] - both[0:AGG] - both[AGG : 2 * AGG]).astype(bf16)
-    for k in (8, 7, -7, 6, -6, 5, -5, 4, -4, 3, -3, 2, -2, 1, -1):
-        sem = vrecv.at[4] if abs(k) <= 4 else vrecv.at[5]
-        send(v2.at[core, slot(0)], v2.at[core, slot(-k)], vsend.at[1], sem, along(k))
+    offer(u2, v2, pb[...] - both[0:AGG] - both[AGG : 2 * AGG], 1)
+    send(u2.at[1 - core], v2.at[part(0, core)], vsend.at[1], vrecv.at[3], along(0, 1 - core))
+    for i in range(DEPTH - 1):
+        target = i + (i + DEPTH - z) // DEPTH
+        place = (z - target + DEPTH) % DEPTH
+        for c in range(2):
+            send(
+                u2.at[c], v2.at[part(place, core)], vsend.at[1], vrecv.at[3],
+                (target * 4 + high * 2 + c, n),
+            )
 
     def prolong(rows):
         value = x1[rows, :] + dot(Pt[rows, :], C[...])
@@ -305,7 +329,7 @@
     over_rows(residual)
     corr = chebyshev(lambda: None)
     trade(corr, t2, n2, tsend.at[1], trecv.at[1])
-    coarse_product(v2, ys2, r2, 4, 8, 5, ysend.at[1], yrecv.at[1], 1)
+    coarse_product(v2, ys2, r2, 31, vrecv.at[3], ysend.at[1], yrecv.at[1], 1)
     wait(n2, trecv.at[1])
 
     def finish(rows):
@@ -313,7 +337,7 @@
         y_ref[rows, :] = x1[rows, :] + value
 
     over_rows(finish)
-    wait(r2.at[pl.ds(0, (GROUP - 1) * AGG)], yrecv.at[1])
+    wait(r2.at[pl.ds(0, (2 * GROUP - 1) * AGG)], yrecv.at[1])
     total = gathered_sum(r2)
     top, low = split(total)
     c_ref[0:AGG, :] = top
@@ -321,15 +345,13 @@
     c_ref[2 * AGG :, :] = jnp.zeros((128 - 2 * AGG, LOADS), bf16)
     coarse_ref[...] = total
 
-    wait(v1.at[core, pl.ds(0, 15 * AGG)], vsend.at[0])
-    wait(aperm.at[0], asem)
+    wait(v1.at[pl.ds(0, 31 * AGG)], vsend.at[0])
+    wait(A2.at[pl.ds(0, 3)], asem)
     wait(t1, tsend.at[0])
-    wait(v1.at[core], csend.at[0])
-    wait(ys1.at[pl.ds(0, (GROUP - 1) * AGG)], ysend.at[0])
-    wait(v2.at[core, pl.ds(0, 15 * AGG)], vsend.at[1])
-    wait(v2.at[core], csend.at[1])
+    wait(ys1.at[pl.ds(0, (2 * GROUP - 1) * AGG)], ysend.at[0])
+    wait(v2.at[pl.ds(0, 31 * AGG)], vsend.at[1])
     wait(t2, tsend.at[1])
-    wait(ys2.at[pl.ds(0, (GROUP - 1) * AGG)], ysend.at[1])
+    wait(ys2.at[pl.ds(0, (2 * GROUP - 1) * AGG)], ysend.at[1])
 
 
 def closing(y_ref, pt_ref, c_ref, coarse_ref, out_ref, out_coarse, ys, osem):
@@ -350,8 +372,8 @@
     anywhere = pl.BlockSpec(memory_space=pl.ANY)
     wide_f32 = pltpu.VMEM((ORDER, LOADS), f32)
     wide_bf16 = pltpu.VMEM((ORDER, LOADS), bf16)
-    square = pltpu.VMEM((CHUNK, LOADS), bf16)
-    pair = pltpu.VMEM((2, CHUNK, LOADS), bf16)
+    pair = pltpu.VMEM((2, AGG, HALF), bf16)
+    tall = pltpu.VMEM((2 * CHUNK, HALF), bf16)
     faces = pltpu.VMEM((4 * FACE, LOADS), bf16)
     hbm = pl.BlockSpec(memory_space=pltpu.HBM)
     dma = pltpu.SemaphoreType.DMA
@@ -381,13 +403,13 @@
             pltpu.VMEM((1, ORDER), jnp.int32),
             pltpu.VMEM((4, FACE), jnp.int32),
             pltpu.VMEM((4, FACE), jnp.int32),
-            pltpu.VMEM((2, 2, 128, CHUNK), bf16),
-            pltpu.VMEM((2, 2, 128, CHUNK), bf16),
-            pair, pair,
-            square, square, square, square, faces, faces, faces, faces,
+            pltpu.VMEM((2, 128, 2 * CHUNK), bf16),
+            pltpu.VMEM((CLASSES, 128, 2 * CHUNK), bf16),
+            pair, pair, tall, tall,
+            tall, tall, tall, tall, faces, faces, faces, faces,
             pltpu.VMEM((128, LOADS), bf16),
             pltpu.VMEM((AGG, LOADS), f32),
-            dma((6,)), dma, dma, dma((2,)), dma((6,)), dma((2,)), dma((2,)),
+            dma((6,)), dma, dma, dma((2,)), dma((4,)),
             dma((2,)), dma((2,)), dma((2,)), dma((2,)),
         ],
         compiler_params=pltpu.CompilerParams(

time: 48.7 us -> 47.3 us (0.971)
  Pallas kernels: 47.9 us -> 46.5 us
    pallas_call x1, Pallas kernels: 46.1 us -> 44.7 us  [local(): pl.pallas_call(kernel, out_shape=(jax.ShapeDtypeStruct((ORDER, LOADS), f3...]
where the time goes in v3:
time: 47.3 us; the launch traced here: 47.1 us
  Pallas kernels  46.5 us (98%)
  between operations  0.64 us (1%)
    pallas_call x1, Pallas kernels, local(): pl.pallas_call(kernel, out_shape=(jax.ShapeDtypeStruct((ORDER, LOADS), f3...  44.7 us
    pallas_call x1, Pallas kernels, local(): pl.pallas_call(closing, out_shape=(jax.ShapeDtypeStruct((ORDER, LOADS), f...  1.82 us

profile of v3, /device:TPU:1, one launch (start us, length us, event | category | flops | bytes accessed | tf_op | source)
XLA Modules:
  0.0 47.1 jit_solution(13922123091829517335)
XLA Ops:
  0.6 44.7 %schwarz.1 = (f32[1024,256]{1,0:T(8,128)S(1)}, bf16[1024,128]{1,0:T(8,128)(2,1)S(1)}, bf16[128,256]{1,0:T(8,128)(2,1)S(1)}, f32[16,256]{1,0:T(8,128)S(1)}) custom-call(bf16[1024,1024]{1,0:T(8,128)(2,1)} %bitcast.5, bf16[1024,256]{1,0:T(8,128)(2,1)} %bitcast.6, bf16[128,1024]{1,0:T(8,128)(2,1)} %inverse.1, s32[4,128]{1,0:T(4,128)} %bitcast.7, ...), custom_call_target="tpu_custom_call" | custom-call | tf_op jit(solution)/shard_map/schwarz/pallas_call | solution.py:380
  45.3 1.8 %closing.1 = (f32[1024,256]{1,0:T(8,128)}, f32[16,256]{1,0:T(8,128)}) custom-call(f32[1024,256]{1,0:T(8,128)S(1)} %get-tuple-element.8.y_ref, bf16[1024,128]{1,0:T(8,128)(2,1)S(1)} %get-tuple-element.9.pt_ref, bf16[128,256]{1,0:T(8,128)(2,1)S(1)} %get-tuple-element.10.c_ref, f32[16,256]{1,0:T(8,128)S(1)} %get-tuple-element.11.coarse_ref), custom_call_target="tpu_custom_call" | custom-call | tf_op jit(solution)/shard_map/closing/pallas_call | solution.py:420

commit v4 on v3

--- a/solution.py
+++ b/solution.py
@@ -207,7 +207,7 @@
                 dst[rows, :] = (new if s < CHEB - 2 else result + new).astype(bf16)
 
             over_rows(step)
-            if s == 1:
+            if s == 0:
                 after_second()
         return db
 

time: 47.3 us -> 46.9 us (level)
  no operation moved by 1% of the time
where the time goes in v4:
time: 46.9 us; the launch traced here: 46.8 us
  Pallas kernels  46.2 us (99%)
  between operations  0.64 us (1%)
    pallas_call x1, Pallas kernels, local(): pl.pallas_call(kernel, out_shape=(jax.ShapeDtypeStruct((ORDER, LOADS), f3...  44.3 us
    pallas_call x1, Pallas kernels, local(): pl.pallas_call(closing, out_shape=(jax.ShapeDtypeStruct((ORDER, LOADS), f...  1.83 us

profile of v4, /device:TPU:1, one launch (start us, length us, event | category | flops | bytes accessed | tf_op | source)
XLA Modules:
  0.0 46.8 jit_solution(4308787324929589083)
XLA Ops:
  0.6 44.3 %schwarz.1 = (f32[1024,256]{1,0:T(8,128)S(1)}, bf16[1024,128]{1,0:T(8,128)(2,1)S(1)}, bf16[128,256]{1,0:T(8,128)(2,1)S(1)}, f32[16,256]{1,0:T(8,128)S(1)}) custom-call(bf16[1024,1024]{1,0:T(8,128)(2,1)} %bitcast.5, bf16[1024,256]{1,0:T(8,128)(2,1)} %bitcast.6, bf16[128,1024]{1,0:T(8,128)(2,1)} %inverse.1, s32[4,128]{1,0:T(4,128)} %bitcast.7, ...), custom_call_target="tpu_custom_call" | custom-call | tf_op jit(solution)/shard_map/schwarz/pallas_call | solution.py:380
  45.0 1.8 %closing.1 = (f32[1024,256]{1,0:T(8,128)}, f32[16,256]{1,0:T(8,128)}) custom-call(f32[1024,256]{1,0:T(8,128)S(1)} %get-tuple-element.8.y_ref, bf16[1024,128]{1,0:T(8,128)(2,1)S(1)} %get-tuple-element.9.pt_ref, bf16[128,256]{1,0:T(8,128)(2,1)S(1)} %get-tuple-element.10.c_ref, f32[16,256]{1,0:T(8,128)S(1)} %get-tuple-element.11.coarse_ref), custom_call_target="tpu_custom_call" | custom-call | tf_op jit(solution)/shard_map/closing/pallas_call | solution.py:420
